TPU v7x, 32 devices: a whole 2x2x4 slice. The times are simulated.
32 devices in a mesh: chan: 4 (over y, core), blk: 8 (over z, x).
Axes of the slice: x: 2, y: 2, z: 4, core: 2. Of those that a mesh axis runs over, the one named last changes fastest.
Arguments:
- comp_alms: float32 [3, 4, 8, 4096], P(None, None, 'blk', 'chan'), may hold values from -6 to 6
- legendre: bfloat16 [2, 8, 4096, 32], P(None, 'blk'), may hold values from -0.09375 to 0.09375
- inv_noise: float32 [4, 2, 32, 8192], P('chan', None, 'blk'), may hold values from 0.5 to 5
- beam_window: float32 [4, 4096], replicated, may hold values from 0.1 to 1
- mixing: float32 [4, 3], replicated, may hold values from 0.2 to 1.5
- channel_of: int32 [4], replicated, may hold values from 0 to 3, each once
- m_orders: int32 [8], replicated, may hold values from 0 to 4095, as said below
- cycle_of: int32 [32], replicated, may hold values from 0 to 31, each once
- cycle_pixels: int32 [32], replicated, may hold values from 4 to 8192, as said below
Outputs:
- normal_product: float32 [3, 4, 8, 4096], P(None, None, 'blk', 'chan')
Inputs may be any that keep to these rules, and one draw needn't show every extreme that they name: `m_orders`: the orders are distinct. `cycle_pixels`: each entry is 4 * min(h, 2048, 8192 - h) for some cycle number h of 1 to 8191; at least one entry equals 8192.
All inputs are finite; a program needn't handle non-finite values.
Results may differ from a plain program's by a relative error of at most 0.0022.
Values may be sent and summed in bfloat16 or wider, within the bound.
A program may use at most 128 MiB of HBM per device.

v0:
```python
import math
import jax
import jax.numpy as jnp
from jax import lax
from jax.sharding import PartitionSpec as P


def phase_rows(orders, pix_count, cycle_width):
    columns = jnp.arange(cycle_width, dtype=jnp.int32)
    phase_steps = orders[:, None] * (2 * columns[None, :] + 1) % (2 * pix_count)
    angles = phase_steps.astype(jnp.float32) * (
        jnp.float32(math.pi) / pix_count.astype(jnp.float32)
    )
    return jnp.concatenate([jnp.cos(angles), jnp.sin(angles)], axis=0).astype(jnp.bfloat16)


def combine_forward(plus_sum, minus_sum):
    return jnp.stack(
        [
            plus_sum[:, 0] - minus_sum[:, 3],
            plus_sum[:, 1] + minus_sum[:, 2],
            plus_sum[:, 2] + minus_sum[:, 1],
            plus_sum[:, 3] - minus_sum[:, 0],
        ],
        axis=1,
    )


def twist_grads(cycle_grads):
    return jnp.stack(
        [-cycle_grads[:, 3], cycle_grads[:, 2], cycle_grads[:, 1], -cycle_grads[:, 0]], axis=1
    )


def cycle_work(coeffs, weights, orders, pix_count):
    slots = coeffs.shape[0]
    cycle_width = weights.shape[-1]
    phases = phase_rows(orders, pix_count, cycle_width)
    half_rows = phases.shape[0] // 2
    real_part = coeffs[:, 0::2]
    imag_part = coeffs[:, 1::2]
    stacked = jnp.concatenate([real_part, -imag_part], axis=2).reshape(2 * slots, 2 * half_rows)
    maps = jnp.dot(stacked, phases, preferred_element_type=jnp.float32)
    live_mask = jnp.arange(cycle_width, dtype=jnp.int32) < pix_count
    scaled = jnp.where(live_mask[None, None, :], weights, 0.0) / pix_count.astype(jnp.float32)
    weighted = (scaled.reshape(maps.shape) * maps).astype(jnp.bfloat16)
    returned = lax.dot_general(
        weighted, phases, (((1,), (1,)), ((), ())), preferred_element_type=jnp.float32
    )
    grad_real = returned[:, :half_rows].reshape(slots, 2, half_rows)
    grad_imag = (-returned[:, half_rows:]).reshape(slots, 2, half_rows)
    return (
        jnp.stack([grad_real, grad_imag], axis=2).reshape(slots, 4, half_rows).astype(jnp.bfloat16)
    )


def mix_components(mix_rows, components):
    accum = mix_rows[:, 0, None, None, None] * components[0][None]
    for comp_index in range(1, components.shape[0]):
        accum = accum + mix_rows[:, comp_index, None, None, None] * components[comp_index][None]
    return accum


def body(
    comp_alms,
    legendre,
    inv_noise,
    beam_window,
    mixing,
    channel_of,
    m_orders,
    cycle_of,
    cycle_pixels,
):
    chan_index = lax.axis_index("chan")
    blk_index = lax.axis_index("blk")
    order_dev = comp_alms.shape[2]
    shard_len = comp_alms.shape[3]
    length = legendre.shape[2]
    cycle_total = legendre.shape[3]
    chan_dev = inv_noise.shape[0]
    cycle_dev = inv_noise.shape[2]
    block_len = min(512, length)
    blocks = length // block_len
    own_orders = lax.dynamic_slice_in_dim(m_orders, blk_index * order_dev, order_dev)
    keep_mask = (jnp.arange(length, dtype=jnp.int32)[None, :] >= own_orders[:, None]).astype(
        jnp.float32
    )
    picked = lax.dynamic_slice_in_dim(channel_of, chan_index * chan_dev, chan_dev)
    mix_rows = jnp.take(mixing, picked, axis=0)
    beam_rows = jnp.take(beam_window, picked, axis=0)
    mix_all = jnp.take(mixing, channel_of, axis=0)
    beam_piece = jnp.take(
        lax.dynamic_slice_in_dim(beam_window, chan_index * shard_len, shard_len, 1),
        channel_of,
        axis=0,
    )
    gathered = lax.all_gather(comp_alms, "chan", axis=3, tiled=True)
    mixed_alm = mix_components(mix_rows, gathered)
    chan_alm = (mixed_alm * beam_rows[:, None, None, :] * keep_mask[None, None]).astype(
        jnp.bfloat16
    )
    order = 0
    row_block = chan_alm[:, :, order, :].reshape(chan_dev * 4, length)
    first_block = own_orders[order] // block_len

    def add_block(index, running, row_block=row_block, order=order):
        plus_sum, minus_sum = running
        offset = index * block_len
        segment = lax.dynamic_slice_in_dim(row_block, offset, block_len, 1)
        tables = lax.dynamic_slice(legendre, (0, order, offset, 0), (2, 1, block_len, cycle_total))
        plus_sum = plus_sum + jnp.dot(segment, tables[0, 0], preferred_element_type=jnp.float32)
        minus_sum = minus_sum + jnp.dot(segment, tables[1, 0], preferred_element_type=jnp.float32)
        return (plus_sum, minus_sum)

    zeros_cycle = jnp.zeros((chan_dev * 4, cycle_total), jnp.float32)
    plus_sum, minus_sum = lax.fori_loop(first_block, blocks, add_block, (zeros_cycle, zeros_cycle))
    coeff_list = [
        combine_forward(
            plus_sum.reshape(chan_dev, 4, cycle_total), minus_sum.reshape(chan_dev, 4, cycle_total)
        )
    ]
    cycle_coeffs = jnp.stack(coeff_list, axis=2).astype(jnp.bfloat16)
    slot_coeffs = jnp.take(cycle_coeffs, cycle_of, axis=3)
    by_cycle = lax.all_to_all(slot_coeffs, "blk", split_axis=3, concat_axis=2, tiled=True)
    first_slot = blk_index * cycle_dev

    def per_cycle(index, collected):
        coeffs = lax.dynamic_index_in_dim(by_cycle, index, 3, keepdims=False)
        weights = lax.dynamic_index_in_dim(inv_noise, index, 2, keepdims=False)
        pix_count = cycle_pixels[cycle_of[first_slot + index]]
        result = cycle_work(coeffs, weights, m_orders, pix_count)
        return lax.dynamic_update_index_in_dim(collected, result, index, 3)

    slot_grads = lax.fori_loop(0, cycle_dev, per_cycle, jnp.zeros(by_cycle.shape, jnp.bfloat16))
    returned = lax.all_to_all(slot_grads, "blk", split_axis=2, concat_axis=3, tiled=True)
    inverse = (
        jnp.zeros((cycle_total,), jnp.int32)
        .at[cycle_of]
        .set(jnp.arange(cycle_total, dtype=jnp.int32))
    )
    cycle_grads = jnp.take(returned, inverse, axis=3)
    order = 0
    order_grads = cycle_grads[:, :, order, :]
    twisted = twist_grads(order_grads).reshape(chan_dev * 4, cycle_total)
    straight = order_grads.reshape(chan_dev * 4, cycle_total)
    first_block = own_orders[order] // block_len

    def add_degrees(index, accum, straight=straight, twisted=twisted, order=order):
        offset = index * block_len
        tables = lax.dynamic_slice(legendre, (0, order, offset, 0), (2, 1, block_len, cycle_total))
        segment = lax.dot_general(
            straight, tables[0, 0], (((1,), (1,)), ((), ())), preferred_element_type=jnp.float32
        )
        segment = segment + lax.dot_general(
            twisted, tables[1, 0], (((1,), (1,)), ((), ())), preferred_element_type=jnp.float32
        )
        return lax.dynamic_update_slice_in_dim(accum, segment, offset, 1)

    accum = lax.fori_loop(
        first_block, blocks, add_degrees, jnp.zeros((chan_dev * 4, length), jnp.float32)
    )
    grad_list = [accum.reshape(chan_dev, 4, length)]
    alm_grads = jnp.stack(grad_list, axis=2) * keep_mask[None, None]
    received = lax.all_to_all(alm_grads, "chan", split_axis=3, concat_axis=0, tiled=True)
    beamed = received * beam_piece[:, None, None, :]
    return jnp.einsum("kc,kpml->cpml", mix_all, beamed, precision=lax.Precision.HIGHEST)


def solution(mesh):
    in_specs = (
        P(None, None, "blk", "chan"),
        P(None, "blk", None, None),
        P("chan", None, "blk", None),
        P(),
        P(),
        P(),
        P(),
        P(),
        P(),
    )
    out_specs = P(None, None, "blk", "chan")
    return jax.shard_map(body, mesh=mesh, in_specs=in_specs, out_specs=out_specs, check_vma=False)
```

profile of v0, /device:TPU:8, one launch (start us, length us, event | category | flops | bytes accessed | tf_op | source)
XLA Modules:
  0.0 151.8 jit_solution(12657113365354323406)
XLA Ops:
  0.0 1.2 dynamic_slice.48
  5.2 1.3 dynamic_slice.49
  11.4 5.6 %all_gather.3 = f32[3,4,1,4096]{3,1,2,0:T(4,128)S(1)} all-gather(f32[3,4,1,1024]{3,1,2,0:T(4,128)S(1)} %copy.31), channel_id=1, replica_groups=mesh['chan'=4,'blk'=8] {'chan'}, dimensions={3}, use_global_device_ids=true | all-gather | bytes 245760 | tf_op jit(solution)/shard_map/all_gather | solution.py:98
  17.6 1.9 %fusion.43 = bf16[4,4096]{1,0:T(4,128)(2,1)S(1)} fusion(f32[4096]{0:T(1024)S(1)} %fusion.44, f32[4096]{0:T(1024)S(1)} %bitcast.126, f32[3,4,1,4096]{3,1,2,0:T(4,128)S(1)} %all_gather.3, f32[]{:T(128)} %bitcast.19, f32[]{:T(128)} %bitcast.18, f32[]{:T(128)} %bitcast.17), kind=kLoop, calls=%fused_computation.70 | loop fusion | flops 131072 | bytes 262156 | tf_op jit(solution)/shard_map/reshape;squeeze | solution.py:104
  19.6 8.9 %while.37 = (s32[]{:T(128)}, f32[4,32]{1,0:T(4,128)S(1)}, f32[4,32]{1,0:T(4,128)S(1)}, bf16[4,4096]{1,0:T(4,128)(2,1)S(1)}, bf16[2,1,4096,32]{2,3,1,0:T(8,128)(2...) while((s32[]{:T(128)}, f32[4,32]{1,0:T(4,128)S(1)}, f32[4,32]{1,0:T(4,128)S(1)}, ...), condition=%wide.region_1.2_spmd, body=%wide.region_0.1_spmd.sunk | while | flops 262407 | bytes 81567 | solution.py:117
  30.0 5.3 %all-to-all-start = ((bf16[1,4,1,32]{1,2,0,3:T(2,128)(2,1)}), bf16[1,4,1,32]{1,2,0,3:T(2,128)(2,1)S(1)}, u32[]{:S(2)}, u32[]{:S(2)}) async-start(bf16[1,4,1,32]{1,2,0,3:T(2,128)(2,1)} %copy.34), calls=%async_computation | async-start | bytes 32768 | tf_op jit(solution)/shard_map/all_to_all | solution.py:125
  38.1 2.3 %all-to-all-done = bf16[1,4,1,32]{1,2,0,3:T(2,128)(2,1)S(1)} async-done(((bf16[1,4,1,32]{1,2,0,3:T(2,128)(2,1)}), bf16[1,4,1,32]{1,2,0,3:T(2,128)(2,1)S(1)}, u32[]{:S(2)}, u32[]{:S(2)}) %all-to-all-start) | async-done | bytes 288 | tf_op jit(solution)/shard_map/all_to_all | solution.py:125
  40.5 50.0 %while.38 = (s32[]{:T(128)}, bf16[1,4,8,4]{2,1,3,0:T(4,128)(2,1)S(1)}, s32[]{:T(128)}, s32[32]{0:T(128)}, s32[32]{0:T(128)}, /*index=5*/f32[1,2,4,8192]{3,2,1,0:...) while((s32[]{:T(128)}, ...), condition=%wide.region_3.5_spmd, body=%wide.region_2.4_spmd.sunk | while | flops 2973951 | bytes 806209 | solution.py:135
  40.5 1.2 dynamic_slice.68
  43.7 1.2 dynamic_slice.69
  46.3 4.4 %cosine_convert_fusion.2 = (bf16[8,8192]{1,0:T(8,128)(2,1)S(1)}, bf16[8,8192]{1,0:T(8,128)(2,1)S(1)}) fusion(f32[]{:T(128)S(6)} %div.51, s32[]{:T(128)S(6)} %select_n.210, s32[8192]{0:T(1024)S(1)} %multiply_add_fusion.2, s32[8]{0:T(128)} %get-tuple-element.485, pred[]{:T(512)S(6)} %lt.154), kind=kLoop, calls=%fused_computation.23.clone.1 | loop fusion | flops 786432 | bytes 294953 | tf_op jit(solution)/shard_map/convert.5
  51.4 1.0 constant_dynamic-slice_fusion.4
  53.0 1.2 dynamic_slice.68
  56.2 1.2 dynamic_slice.69
  58.8 4.4 %cosine_convert_fusion.2 = (bf16[8,8192]{1,0:T(8,128)(2,1)S(1)}, bf16[8,8192]{1,0:T(8,128)(2,1)S(1)}) fusion(f32[]{:T(128)S(6)} %div.51, s32[]{:T(128)S(6)} %select_n.210, s32[8192]{0:T(1024)S(1)} %multiply_add_fusion.2, s32[8]{0:T(128)} %get-tuple-element.485, pred[]{:T(512)S(6)} %lt.154), kind=kLoop, calls=%fused_computation.23.clone.1 | loop fusion | flops 786432 | bytes 294953 | tf_op jit(solution)/shard_map/convert.5
  65.5 1.2 dynamic_slice.68
  68.7 1.2 dynamic_slice.69
  71.3 4.4 %cosine_convert_fusion.2 = (bf16[8,8192]{1,0:T(8,128)(2,1)S(1)}, bf16[8,8192]{1,0:T(8,128)(2,1)S(1)}) fusion(f32[]{:T(128)S(6)} %div.51, s32[]{:T(128)S(6)} %select_n.210, s32[8192]{0:T(1024)S(1)} %multiply_add_fusion.2, s32[8]{0:T(128)} %get-tuple-element.485, pred[]{:T(512)S(6)} %lt.154), kind=kLoop, calls=%fused_computation.23.clone.1 | loop fusion | flops 786432 | bytes 294953 | tf_op jit(solution)/shard_map/convert.5
  76.4 1.0 constant_dynamic-slice_fusion.4
  78.0 1.2 dynamic_slice.68
  81.2 1.2 dynamic_slice.69
  83.8 4.4 %cosine_convert_fusion.2 = (bf16[8,8192]{1,0:T(8,128)(2,1)S(1)}, bf16[8,8192]{1,0:T(8,128)(2,1)S(1)}) fusion(f32[]{:T(128)S(6)} %div.51, s32[]{:T(128)S(6)} %select_n.210, s32[8192]{0:T(1024)S(1)} %multiply_add_fusion.2, s32[8]{0:T(128)} %get-tuple-element.485, pred[]{:T(512)S(6)} %lt.154), kind=kLoop, calls=%fused_computation.23.clone.1 | loop fusion | flops 786432 | bytes 294953 | tf_op jit(solution)/shard_map/convert.5
  91.2 4.8 %all-to-all-start.1 = ((bf16[1,4,8,4]{1,3,0,2:T(4,128)(2,1)}), bf16[1,4,8,4]{1,3,0,2:T(4,128)(2,1)S(1)}, u32[]{:S(2)}, u32[]{:S(2)}) async-start(bf16[1,4,8,4]{1,3,0,2:T(4,128)(2,1)} %copy.38), calls=%async_computation.1 | async-start | bytes 16384 | tf_op jit(solution)/shard_map/all_to_all | solution.py:136
  96.6 4.5 %all-to-all-done.1 = bf16[1,4,8,4]{1,3,0,2:T(4,128)(2,1)S(1)} async-done(((bf16[1,4,8,4]{1,3,0,2:T(4,128)(2,1)}), bf16[1,4,8,4]{1,3,0,2:T(4,128)(2,1)S(1)}, u32[]{:S(2)}, u32[]{:S(2)}) %all-to-all-start.1) | async-done | bytes 288 | tf_op jit(solution)/shard_map/all_to_all | solution.py:136
  101.8 8.8 %while.39 = (s32[]{:T(128)}, f32[4,4096]{1,0:T(4,128)S(1)}, bf16[2,1,4096,32]{2,3,1,0:T(8,128)(2,1)}, bf16[4,32]{1,0:T(4,128)(2,1)S(1)}, bf16[4,32]{1,0:T(4,128)...) while((s32[]{:T(128)}, f32[4,4096]{1,0:T(4,128)S(1)}, ...), condition=%wide.region_6.8_spmd, body=%wide.region_5.7_spmd.sunk | while | flops 264199 | bytes 93091 | solution.py:160
  110.6 2.0 %copy.42 = f32[4,4096]{0,1:T(8,128)} copy(f32[4,4096]{1,0:T(4,128)S(1)} %get-tuple-element.203) | data formatting | bytes 131072 | tf_op jit(solution)/shard_map/while | solution.py:160
  112.6 2.2 %broadcast_multiply_fusion = f32[4,4096]{0,1:T(8,128)S(1)} fusion(f32[4,4096]{0,1:T(8,128)} %copy.42, f32[4096]{0:T(1024)S(1)} %fusion.44), kind=kLoop, calls=%fused_computation.58 | loop fusion | flops 16384 | bytes 147456 | tf_op jit(solution)/shard_map/mul | solution.py:164
  115.3 19.4 %reduce = f32[4096,4]{1,0:T(8,128)} reduce(f32[4096,1,1,4]{3,2,1,0:T(1,128)S(1)} %bitcast.121, f32[]{:T(128)} %broadcast.233), dimensions={1,2}, to_apply=%bitcast.83.reduce_sub_computation | reduce | bytes 131076
  134.7 3.9 %reshape.357 = f32[4,1,4096]{2,1,0:T(1,128)} reshape(f32[4096,4]{1,0:T(8,128)} %reduce) | data formatting | bytes 131072
  138.6 3.5 %all-to-all-start.2 = ((f32[4,1,4096]{2,1,0:T(1,128)}), f32[4,1,4096]{2,1,0:T(1,128)S(1)}, u32[]{:S(2)}, u32[]{:S(2)}) async-start(f32[4,1,4096]{2,1,0:T(1,128)} %reshape.357), calls=%async_computation.2 | async-start | bytes 131072 | tf_op jit(solution)/shard_map/all_to_all | solution.py:165
  142.7 3.3 %all-to-all-done.2 = f32[4,1,4096]{2,1,0:T(1,128)S(1)} async-done(((f32[4,1,4096]{2,1,0:T(1,128)}), f32[4,1,4096]{2,1,0:T(1,128)S(1)}, u32[]{:S(2)}, u32[]{:S(2)}) %all-to-all-start.2) | async-done | bytes 65568 | tf_op jit(solution)/shard_map/all_to_all | solution.py:165
  146.8 3.3 %reshape.358 = f32[4096,1,1,4]{3,2,1,0:T(1,128)S(1)} reshape(f32[4,4096]{1,0:T(4,128)S(1)} %reduce.1) | data formatting | bytes 131072
  (116 shorter events, 39.8 us)
Async XLA Ops:
  30.0 10.4 %all-to-all-start = ((bf16[1,4,1,32]{1,2,0,3:T(2,128)(2,1)}), bf16[1,4,1,32]{1,2,0,3:T(2,128)(2,1)S(1)}, u32[]{:S(2)}, u32[]{:S(2)}) async-start(bf16[1,4,1,32]{1,2,0,3:T(2,128)(2,1)} %copy.34), calls=%async_computation | async-start | bytes 32768 | tf_op jit(solution)/shard_map/all_to_all | solution.py:125
  91.2 9.8 %all-to-all-start.1 = ((bf16[1,4,8,4]{1,3,0,2:T(4,128)(2,1)}), bf16[1,4,8,4]{1,3,0,2:T(4,128)(2,1)S(1)}, u32[]{:S(2)}, u32[]{:S(2)}) async-start(bf16[1,4,8,4]{1,3,0,2:T(4,128)(2,1)} %copy.38), calls=%async_computation.1 | async-start | bytes 16384 | tf_op jit(solution)/shard_map/all_to_all | solution.py:136
  134.7 7.5 %copy-start = (f32[4,3]{1,0:T(4,128)S(1)}, f32[4,3]{1,0:T(4,128)}, u32[]{:S(2)}) copy-start(f32[4,3]{1,0:T(4,128)} %param.21) | copy-start | bytes 148
  138.6 7.4 %all-to-all-start.2 = ((f32[4,1,4096]{2,1,0:T(1,128)}), f32[4,1,4096]{2,1,0:T(1,128)S(1)}, u32[]{:S(2)}, u32[]{:S(2)}) async-start(f32[4,1,4096]{2,1,0:T(1,128)} %reshape.357), calls=%async_computation.2 | async-start | bytes 131072 | tf_op jit(solution)/shard_map/all_to_all | solution.py:165
where the time goes:
time: 154 us; the launch traced here: 152 us
  other arithmetic  49.9 us (32%)
  local copies, waits for them, and re-layouts  34.9 us (23%)
  matrix products  19.7 us (13%)
  starting transfers between devices  13.6 us (9%)
  loops' own time  13.5 us (9%)
  waiting for transfers between devices  10 us (6%)
  blocking collectives  5.6 us (4%)
  between operations  4.67 us (3%)
    unnamed x1, other arithmetic  19.4 us
    another operation x5, other arithmetic  17.5 us
    another operation x1, loops' own time, body(): lax.fori_loop(0, cycle_dev, per_cycle, jnp.zeros(by_cycle.shape, jnp.bflo...  13.4 us
    dynamic_slice x8, local copies, waits for them, and re-layouts, per_cycle(): pix_count = cycle_pixels[cycle_of[first_slot + index]]  9.93 us
    unnamed x7, local copies, waits for them, and re-layouts  8.55 us
    all_gather x1, blocking collectives, body(): gathered = lax.all_gather(comp_alms, 'chan', axis=3, tiled=True)  5.6 us
    all_to_all x1, starting transfers between devices, body(): lax.all_to_all(slot_coeffs, 'blk', split_axis=3, concat_axis=2, tiled=True)  5.32 us
    all_to_all x1, starting transfers between devices, body(): lax.all_to_all(slot_grads, 'blk', split_axis=2, concat_axis=3, tiled=True)  4.79 us
  transfers between devices with their start and end apart: 3, of which 3 were waited for; matrix products, arithmetic and copies ran while one was open for 3% of the time, Pallas kernels for 0%

commit v1 on v0

--- a/solution.py
+++ b/solution.py
@@ -3,6 +3,21 @@
 import jax.numpy as jnp
 from jax import lax
 from jax.sharding import PartitionSpec as P
+from jax.lax import axis_index, ppermute, psum
+
+
+def state_ratios(piece_in, array_axis, arr):
+    prior = piece_in.shape
+    carry_out = piece_in.reshape(
+        *prior[:array_axis], arr, prior[array_axis] // arr, *prior[array_axis + 1 :]
+    )
+    return jnp.moveaxis(carry_out, array_axis, 0)
+
+
+def part_the_scales(u, axis_no):
+    raw_out = list(u.shape[1:])
+    raw_out[axis_no] *= u.shape[0]
+    return jnp.moveaxis(u, 0, axis_no).reshape(raw_out)
 
 
 def phase_rows(orders, pix_count, cycle_width):
@@ -133,7 +148,18 @@
         return lax.dynamic_update_index_in_dim(collected, result, index, 3)
 
     slot_grads = lax.fori_loop(0, cycle_dev, per_cycle, jnp.zeros(by_cycle.shape, jnp.bfloat16))
-    returned = lax.all_to_all(slot_grads, "blk", split_axis=2, concat_axis=3, tiled=True)
+    g_now = psum(1, "blk")
+    high = axis_index("blk")
+    part_now, right_arr = (g_now, high)
+    opened = state_ratios(slot_grads, 2, part_now)
+    entries = [opened[right_arr]]
+    for dev_i in range(1, part_now):
+        block_next = opened[(right_arr + dev_i) % part_now]
+        plain = ppermute(block_next, "blk", [(q, (q + dev_i) % part_now) for q in range(part_now)])
+        entries.append(plain)
+    parts_out = jnp.stack(entries, axis=0)
+    opened = parts_out[(right_arr - jnp.arange(part_now)) % part_now]
+    returned = part_the_scales(opened, 3)
     inverse = (
         jnp.zeros((cycle_total,), jnp.int32)
         .at[cycle_of]

time: 154 us -> 158 us (1.026)
  starting transfers between devices: 13.6 us -> 19.6 us
  waiting for transfers between devices: 10 us -> 6.38 us
    ppermute x0 -> x7, starting transfers between devices: none -> 10.8 us  [body(): ppermute(block_next, 'blk', [(q, (q + dev_i) % part_now) for q in range(p...]
    all_to_all x1 -> x0, starting transfers between devices: 4.79 us -> none  [body(): lax.all_to_all(slot_grads, 'blk', split_axis=2, concat_axis=3, tiled=True)]
    all_to_all x1 -> x0, waiting for transfers between devices: 4.48 us -> none  [body(): lax.all_to_all(slot_grads, 'blk', split_axis=2, concat_axis=3, tiled=True)]
    unnamed x7 -> x14, local copies, waits for them, and re-layouts: 8.55 us -> 8.61 us
  transfers between devices with their start and end apart: 3 -> 9, of which waited for: 3 -> 4; matrix products, arithmetic and copies ran while one was open for 3% -> 3% of each run, Pallas kernels for 0% -> 0%
where the time goes in v1:
time: 158 us; the launch traced here: 156 us
  other arithmetic  49.9 us (32%)
  local copies, waits for them, and re-layouts  36.2 us (23%)
  matrix products  19.7 us (12%)
  starting transfers between devices  19.6 us (12%)
  loops' own time  13.5 us (9%)
  waiting for transfers between devices  6.38 us (4%)
  blocking collectives  5.6 us (4%)
  between operations  4.91 us (3%)
    unnamed x1, other arithmetic  19.4 us
    another operation x5, other arithmetic  17.5 us
    another operation x1, loops' own time, body(): lax.fori_loop(0, cycle_dev, per_cycle, jnp.zeros(by_cycle.shape, jnp.bflo...  13.4 us
    ppermute x7, starting transfers between devices, body(): ppermute(block_next, 'blk', [(q, (q + dev_i) % part_now) for q in range(p...  10.8 us
    dynamic_slice x8, local copies, waits for them, and re-layouts, per_cycle(): pix_count = cycle_pixels[cycle_of[first_slot + index]]  9.93 us
    unnamed x14, local copies, waits for them, and re-layouts  8.61 us
    all_gather x1, blocking collectives, body(): gathered = lax.all_gather(comp_alms, 'chan', axis=3, tiled=True)  5.6 us
    all_to_all x1, starting transfers between devices, body(): lax.all_to_all(slot_coeffs, 'blk', split_axis=3, concat_axis=2, tiled=True)  5.32 us
  transfers between devices with their start and end apart: 9, of which 4 were waited for; matrix products, arithmetic and copies ran while one was open for 3% of the time, Pallas kernels for 0%

profile of v1, /device:TPU:8, one launch (start us, length us, event | category | flops | bytes accessed | tf_op | source)
XLA Modules:
  0.0 155.7 jit_solution(13076562199894040492)
XLA Ops:
  0.0 1.2 dynamic_slice.58
  5.2 1.3 dynamic_slice.59
  11.6 5.6 %all_gather.3 = f32[3,4,1,4096]{3,1,2,0:T(4,128)S(1)} all-gather(f32[3,4,1,1024]{3,1,2,0:T(4,128)S(1)} %copy.51), channel_id=1, replica_groups=mesh['chan'=4,'blk'=8] {'chan'}, dimensions={3}, use_global_device_ids=true | all-gather | bytes 245760 | tf_op jit(solution)/shard_map/all_gather | solution.py:113
  17.9 1.9 %fusion.43 = bf16[4,4096]{1,0:T(4,128)(2,1)S(1)} fusion(f32[4096]{0:T(1024)S(1)} %fusion.44, f32[4096]{0:T(1024)S(1)} %bitcast.146, f32[3,4,1,4096]{3,1,2,0:T(4,128)S(1)} %all_gather.3, f32[]{:T(128)} %bitcast.19, f32[]{:T(128)} %bitcast.18, f32[]{:T(128)} %bitcast.17), kind=kLoop, calls=%fused_computation.71 | loop fusion | flops 131072 | bytes 262156 | tf_op jit(solution)/shard_map/reshape;squeeze | solution.py:119
  19.8 8.9 %while.37 = (s32[]{:T(128)}, f32[4,32]{1,0:T(4,128)S(1)}, f32[4,32]{1,0:T(4,128)S(1)}, bf16[4,4096]{1,0:T(4,128)(2,1)S(1)}, bf16[2,1,4096,32]{2,3,1,0:T(8,128)(2...) while((s32[]{:T(128)}, f32[4,32]{1,0:T(4,128)S(1)}, f32[4,32]{1,0:T(4,128)S(1)}, ...), condition=%wide.region_1.2_spmd, body=%wide.region_0.1_spmd.sunk | while | flops 262407 | bytes 81567 | solution.py:132
  30.3 5.3 %all-to-all-start = ((bf16[1,4,1,32]{1,2,0,3:T(2,128)(2,1)}), bf16[1,4,1,32]{1,2,0,3:T(2,128)(2,1)S(1)}, u32[]{:S(2)}, u32[]{:S(2)}) async-start(bf16[1,4,1,32]{1,2,0,3:T(2,128)(2,1)} %copy.54), calls=%async_computation | async-start | bytes 32768 | tf_op jit(solution)/shard_map/all_to_all | solution.py:140
  39.0 1.6 %all-to-all-done = bf16[1,4,1,32]{1,2,0,3:T(2,128)(2,1)S(1)} async-done(((bf16[1,4,1,32]{1,2,0,3:T(2,128)(2,1)}), bf16[1,4,1,32]{1,2,0,3:T(2,128)(2,1)S(1)}, u32[]{:S(2)}, u32[]{:S(2)}) %all-to-all-start) | async-done | bytes 288 | tf_op jit(solution)/shard_map/all_to_all | solution.py:140
  40.7 50.0 %while.38 = (s32[]{:T(128)}, bf16[1,4,8,4]{2,1,3,0:T(4,128)(2,1)S(1)}, s32[]{:T(128)}, s32[32]{0:T(128)}, s32[32]{0:T(128)}, /*index=5*/f32[1,2,4,8192]{3,2,1,0:...) while((s32[]{:T(128)}, ...), condition=%wide.region_3.5_spmd, body=%wide.region_2.4_spmd.sunk | while | flops 2973951 | bytes 806209 | solution.py:150
  40.7 1.2 dynamic_slice.79
  43.9 1.2 dynamic_slice.80
  46.5 4.4 %cosine_convert_fusion.2 = (bf16[8,8192]{1,0:T(8,128)(2,1)S(1)}, bf16[8,8192]{1,0:T(8,128)(2,1)S(1)}) fusion(f32[]{:T(128)S(6)} %div.51, s32[]{:T(128)S(6)} %select_n.309, s32[8192]{0:T(1024)S(1)} %multiply_add_fusion.2, s32[8]{0:T(128)} %get-tuple-element.495, pred[]{:T(512)S(6)} %lt.246), kind=kLoop, calls=%fused_computation.24.clone.1 | loop fusion | flops 786432 | bytes 294953 | tf_op jit(solution)/shard_map/convert.5
  51.6 1.0 constant_dynamic-slice_fusion.12
  53.2 1.2 dynamic_slice.79
  56.4 1.2 dynamic_slice.80
  59.0 4.4 %cosine_convert_fusion.2 = (bf16[8,8192]{1,0:T(8,128)(2,1)S(1)}, bf16[8,8192]{1,0:T(8,128)(2,1)S(1)}) fusion(f32[]{:T(128)S(6)} %div.51, s32[]{:T(128)S(6)} %select_n.309, s32[8192]{0:T(1024)S(1)} %multiply_add_fusion.2, s32[8]{0:T(128)} %get-tuple-element.495, pred[]{:T(512)S(6)} %lt.246), kind=kLoop, calls=%fused_computation.24.clone.1 | loop fusion | flops 786432 | bytes 294953 | tf_op jit(solution)/shard_map/convert.5
  65.7 1.2 dynamic_slice.79
  68.9 1.2 dynamic_slice.80
  71.5 4.4 %cosine_convert_fusion.2 = (bf16[8,8192]{1,0:T(8,128)(2,1)S(1)}, bf16[8,8192]{1,0:T(8,128)(2,1)S(1)}) fusion(f32[]{:T(128)S(6)} %div.51, s32[]{:T(128)S(6)} %select_n.309, s32[8192]{0:T(1024)S(1)} %multiply_add_fusion.2, s32[8]{0:T(128)} %get-tuple-element.495, pred[]{:T(512)S(6)} %lt.246), kind=kLoop, calls=%fused_computation.24.clone.1 | loop fusion | flops 786432 | bytes 294953 | tf_op jit(solution)/shard_map/convert.5
  78.2 1.2 dynamic_slice.79
  81.4 1.2 dynamic_slice.80
  84.0 4.4 %cosine_convert_fusion.2 = (bf16[8,8192]{1,0:T(8,128)(2,1)S(1)}, bf16[8,8192]{1,0:T(8,128)(2,1)S(1)}) fusion(f32[]{:T(128)S(6)} %div.51, s32[]{:T(128)S(6)} %select_n.309, s32[8192]{0:T(1024)S(1)} %multiply_add_fusion.2, s32[8]{0:T(128)} %get-tuple-element.495, pred[]{:T(512)S(6)} %lt.246), kind=kLoop, calls=%fused_computation.24.clone.1 | loop fusion | flops 786432 | bytes 294953 | tf_op jit(solution)/shard_map/convert.5
  92.3 4.1 %collective-permute-start.2 = (bf16[1,4,1,4]{2,1,3,0:T(4,128)(2,1)S(1)}, bf16[1,4,1,4]{2,1,3,0:T(4,128)(2,1)S(1)}, u32[]{:S(2)}, u32[]{:S(2)}) collective-permute-start(bf16[1,4,1,4]{2,1,3,0:T(4,128)(2,1)S(1)} %get-tuple-element.294), channel_id=1, source_target_pairs={{0,3},{1,4},{2,5},{3,6},{4,7},{5,0},{6,1},{7,2},{8,11},{9,12},{10,... | collective-permute-start | bytes 104 | tf_op jit(solution)/shard_map/ppermute | solution.py:158
  97.0 2.3 %collective-permute-start.4 = (bf16[1,4,1,4]{2,1,3,0:T(4,128)(2,1)S(1)}, bf16[1,4,1,4]{2,1,3,0:T(4,128)(2,1)S(1)}, u32[]{:S(2)}, u32[]{:S(2)}) collective-permute-start(bf16[1,4,1,4]{2,1,3,0:T(4,128)(2,1)S(1)} %get-tuple-element.292), channel_id=1, source_target_pairs={{0,5},{1,6},{2,7},{3,0},{4,1},{5,2},{6,3},{7,4},{8,13},{9,14},{10,... | collective-permute-start | bytes 104 | tf_op jit(solution)/shard_map/ppermute | solution.py:158
  99.4 2.4 %collective-permute-start.6 = (bf16[1,4,1,4]{2,1,3,0:T(4,128)(2,1)S(1)}, bf16[1,4,1,4]{2,1,3,0:T(4,128)(2,1)S(1)}, u32[]{:S(2)}, u32[]{:S(2)}) collective-permute-start(bf16[1,4,1,4]{2,1,3,0:T(4,128)(2,1)S(1)} %get-tuple-element.290), channel_id=1, source_target_pairs={{0,7},{1,0},{2,1},{3,2},{4,3},{5,4},{6,5},{7,6},{8,15},{9,8},{10,9... | collective-permute-start | bytes 104 | tf_op jit(solution)/shard_map/ppermute | solution.py:158
  105.7 8.8 %while.39 = (s32[]{:T(128)}, f32[4,4096]{1,0:T(4,128)S(1)}, bf16[2,1,4096,32]{2,3,1,0:T(8,128)(2,1)}, bf16[4,32]{1,0:T(4,128)(2,1)S(1)}, bf16[4,32]{1,0:T(4,128)...) while((s32[]{:T(128)}, f32[4,4096]{1,0:T(4,128)S(1)}, ...), condition=%wide.region_6.8_spmd, body=%wide.region_5.7_spmd.sunk | while | flops 264199 | bytes 93091 | solution.py:186
  114.6 2.0 %copy.72 = f32[4,4096]{0,1:T(8,128)} copy(f32[4,4096]{1,0:T(4,128)S(1)} %get-tuple-element.203) | data formatting | bytes 131072 | tf_op jit(solution)/shard_map/while | solution.py:186
  116.5 2.2 %broadcast_multiply_fusion = f32[4,4096]{0,1:T(8,128)S(1)} fusion(f32[4,4096]{0,1:T(8,128)} %copy.72, f32[4096]{0:T(1024)S(1)} %fusion.44), kind=kLoop, calls=%fused_computation.59 | loop fusion | flops 16384 | bytes 147456 | tf_op jit(solution)/shard_map/mul | solution.py:190
  119.3 19.4 %reduce = f32[4096,4]{1,0:T(8,128)} reduce(f32[4096,1,1,4]{3,2,1,0:T(1,128)S(1)} %bitcast.141, f32[]{:T(128)} %broadcast.309), dimensions={1,2}, to_apply=%bitcast.103.reduce_sub_computation | reduce | bytes 131076
  138.6 3.9 %reshape.454 = f32[4,1,4096]{2,1,0:T(1,128)} reshape(f32[4096,4]{1,0:T(8,128)} %reduce) | data formatting | bytes 131072
  142.5 3.5 %all-to-all-start.1 = ((f32[4,1,4096]{2,1,0:T(1,128)}), f32[4,1,4096]{2,1,0:T(1,128)S(1)}, u32[]{:S(2)}, u32[]{:S(2)}) async-start(f32[4,1,4096]{2,1,0:T(1,128)} %reshape.454), calls=%async_computation.1 | async-start | bytes 131072 | tf_op jit(solution)/shard_map/all_to_all | solution.py:191
  146.6 3.3 %all-to-all-done.1 = f32[4,1,4096]{2,1,0:T(1,128)S(1)} async-done(((f32[4,1,4096]{2,1,0:T(1,128)}), f32[4,1,4096]{2,1,0:T(1,128)S(1)}, u32[]{:S(2)}, u32[]{:S(2)}) %all-to-all-start.1) | async-done | bytes 65568 | tf_op jit(solution)/shard_map/all_to_all | solution.py:191
  150.7 3.3 %reshape.455 = f32[4096,1,1,4]{3,2,1,0:T(1,128)S(1)} reshape(f32[4,4096]{1,0:T(4,128)S(1)} %reduce.1) | data formatting | bytes 131072
  (148 shorter events, 45.5 us)
Async XLA Ops:
  30.3 10.4 %all-to-all-start = ((bf16[1,4,1,32]{1,2,0,3:T(2,128)(2,1)}), bf16[1,4,1,32]{1,2,0,3:T(2,128)(2,1)S(1)}, u32[]{:S(2)}, u32[]{:S(2)}) async-start(bf16[1,4,1,32]{1,2,0,3:T(2,128)(2,1)} %copy.54), calls=%async_computation | async-start | bytes 32768 | tf_op jit(solution)/shard_map/all_to_all | solution.py:140
  90.8 8.5 %collective-permute-start = (bf16[1,4,1,4]{2,1,3,0:T(4,128)(2,1)S(1)}, bf16[1,4,1,4]{2,1,3,0:T(4,128)(2,1)S(1)}, u32[]{:S(2)}, u32[]{:S(2)}) collective-permute-start(bf16[1,4,1,4]{2,1,3,0:T(4,128)(2,1)S(1)} %get-tuple-element.296), channel_id=1, source_target_pairs={{0,1},{1,2},{2,3},{3,4},{4,5},{5,6},{6,7},{7,0},{8,9},{9,10},{10,1... | collective-permute-start | bytes 104 | tf_op jit(solution)/shard_map/ppermute | solution.py:158
  91.7 7.8 %collective-permute-start.1 = (bf16[1,4,1,4]{2,1,3,0:T(4,128)(2,1)S(1)}, bf16[1,4,1,4]{2,1,3,0:T(4,128)(2,1)S(1)}, u32[]{:S(2)}, u32[]{:S(2)}) collective-permute-start(bf16[1,4,1,4]{2,1,3,0:T(4,128)(2,1)S(1)} %get-tuple-element.295), channel_id=1, source_target_pairs={{0,2},{1,3},{2,4},{3,5},{4,6},{5,7},{6,0},{7,1},{8,10},{9,11},{10,... | collective-permute-start | bytes 104 | tf_op jit(solution)/shard_map/ppermute | solution.py:158
  92.3 9.7 %collective-permute-start.2 = (bf16[1,4,1,4]{2,1,3,0:T(4,128)(2,1)S(1)}, bf16[1,4,1,4]{2,1,3,0:T(4,128)(2,1)S(1)}, u32[]{:S(2)}, u32[]{:S(2)}) collective-permute-start(bf16[1,4,1,4]{2,1,3,0:T(4,128)(2,1)S(1)} %get-tuple-element.294), channel_id=1, source_target_pairs={{0,3},{1,4},{2,5},{3,6},{4,7},{5,0},{6,1},{7,2},{8,11},{9,12},{10,... | collective-permute-start | bytes 104 | tf_op jit(solution)/shard_map/ppermute | solution.py:158
  96.4 5.7 %collective-permute-start.3 = (bf16[1,4,1,4]{2,1,3,0:T(4,128)(2,1)S(1)}, bf16[1,4,1,4]{2,1,3,0:T(4,128)(2,1)S(1)}, u32[]{:S(2)}, u32[]{:S(2)}) collective-permute-start(bf16[1,4,1,4]{2,1,3,0:T(4,128)(2,1)S(1)} %get-tuple-element.293), channel_id=1, source_target_pairs={{0,4},{1,5},{2,6},{3,7},{4,0},{5,1},{6,2},{7,3},{8,12},{9,13},{10,... | collective-permute-start | bytes 104 | tf_op jit(solution)/shard_map/ppermute | solution.py:158
  97.0 5.3 %collective-permute-start.4 = (bf16[1,4,1,4]{2,1,3,0:T(4,128)(2,1)S(1)}, bf16[1,4,1,4]{2,1,3,0:T(4,128)(2,1)S(1)}, u32[]{:S(2)}, u32[]{:S(2)}) collective-permute-start(bf16[1,4,1,4]{2,1,3,0:T(4,128)(2,1)S(1)} %get-tuple-element.292), channel_id=1, source_target_pairs={{0,5},{1,6},{2,7},{3,0},{4,1},{5,2},{6,3},{7,4},{8,13},{9,14},{10,... | collective-permute-start | bytes 104 | tf_op jit(solution)/shard_map/ppermute | solution.py:158
  99.3 3.6 %collective-permute-start.5 = (bf16[1,4,1,4]{2,1,3,0:T(4,128)(2,1)S(1)}, bf16[1,4,1,4]{2,1,3,0:T(4,128)(2,1)S(1)}, u32[]{:S(2)}, u32[]{:S(2)}) collective-permute-start(bf16[1,4,1,4]{2,1,3,0:T(4,128)(2,1)S(1)} %get-tuple-element.291), channel_id=1, source_target_pairs={{0,6},{1,7},{2,0},{3,1},{4,2},{5,3},{6,4},{7,5},{8,14},{9,15},{10,... | collective-permute-start | bytes 104 | tf_op jit(solution)/shard_map/ppermute | solution.py:158
  99.4 4.6 %collective-permute-start.6 = (bf16[1,4,1,4]{2,1,3,0:T(4,128)(2,1)S(1)}, bf16[1,4,1,4]{2,1,3,0:T(4,128)(2,1)S(1)}, u32[]{:S(2)}, u32[]{:S(2)}) collective-permute-start(bf16[1,4,1,4]{2,1,3,0:T(4,128)(2,1)S(1)} %get-tuple-element.290), channel_id=1, source_target_pairs={{0,7},{1,0},{2,1},{3,2},{4,3},{5,4},{6,5},{7,6},{8,15},{9,8},{10,9... | collective-permute-start | bytes 104 | tf_op jit(solution)/shard_map/ppermute | solution.py:158
  138.6 7.5 %copy-start = (f32[4,3]{1,0:T(4,128)S(1)}, f32[4,3]{1,0:T(4,128)}, u32[]{:S(2)}) copy-start(f32[4,3]{1,0:T(4,128)} %param.21) | copy-start | bytes 148
  142.5 7.4 %all-to-all-start.1 = ((f32[4,1,4096]{2,1,0:T(1,128)}), f32[4,1,4096]{2,1,0:T(1,128)S(1)}, u32[]{:S(2)}, u32[]{:S(2)}) async-start(f32[4,1,4096]{2,1,0:T(1,128)} %reshape.454), calls=%async_computation.1 | async-start | bytes 131072 | tf_op jit(solution)/shard_map/all_to_all | solution.py:191
